TPU v7x, 32 devices: a whole 2x2x4 slice. The times are simulated.
32 devices in a mesh: blk: 32 (over z, y, x, core).
Axes of the slice: x: 2, y: 2, z: 4, core: 2. Of those that a mesh axis runs over, the one named last changes fastest.
Arguments:
- old_phase: float32 [512, 32768], P('blk'), may hold values from -1 to 1
- old_solute: float32 [512, 32768], P('blk'), may hold values from -0.45 to 0.45
- old_mobility: float32 [512, 32768], P('blk'), may hold values from 0.25 to 1
- new_global_slot: int32 [512], P('blk'), may hold values from -1 to 255, as said below
- neighbors: int32 [256, 6], P('blk'), may hold values from -1 to 255, as said below
Outputs:
- phase: float32 [256, 32768], P('blk')
- solute: float32 [256, 32768], P('blk')
Inputs may be any that keep to these rules, and one draw needn't show every extreme that they name: Each device's old slots hold its blocks first and -1 after them; the blocks taken in device order and slot order get the consecutive numbers 0 to 255. The block in an old slot of device p goes to device new_global_slot // 8, at most 2 devices away; in every draw some block moves exactly 2 devices down and some exactly 2 up, some device holds 16 blocks and some none. `neighbors`: the relation is symmetric: if b is the +x (+y, +z) neighbour of a, then a is the -x (-y, -z) neighbour of b. The x neighbours of a block of device p lie on devices p - 1 and p + 1 (every block has both except on the first and last device, where that side is -1); y and z neighbours lie on the block's own device, with -1 at the ends along y and none along z (a block may be its own z neighbour). The layers of blocks line up: if b is the -x (+x) neighbour of a, then the y and z neighbours of b are the -x (+x) neighbours of the y and z neighbours of a, and -1 where those are -1.
All inputs are finite; a program needn't handle non-finite values.
Results may differ from a plain program's by a relative error of at most 0.00014.
Values sent between devices are 32-bit elements; how exact they have to be, the bound alone decides.
A program may use at most 128 MiB of HBM per device.

v0:
```python
import functools

import jax
import jax.numpy as jnp
from jax import lax
from jax.experimental import pallas as pl
from jax.experimental.pallas import tpu as pltpu
from jax.sharding import PartitionSpec as P

EDGE = 32
STEPS = 3
FIELDS = 3
SUB = 8
LANES = 128
LAG = 3

time_step = 0.15
coupling = 1.5


def kernel(n, cap, nold, ngs, nbs, op, oc, om, phi_out, conc_out, old,
           side_s, side_r, pair_s, pair_r, far_s, far_r, near_s, near_r,
           fld, mob, ghost0, ghost1, ghost2, lsem, ssem, rsem, hs, hr):
    ghosts = (ghost0, ghost1, ghost2)
    rows = EDGE * SUB
    span = nold * rows
    items = FIELDS * cap
    loads = [
        pltpu.make_async_copy(src, old.at[pl.ds(f * span, span)], lsem.at[f])
        for f, src in enumerate((op, oc, om))
    ]
    for copy in loads:
        copy.start()

    me = lax.axis_index("blk")
    core = me % 2
    odd = (me // 2) % 2
    sib = me + 1 - 2 * core
    near = me + 2 - 4 * odd
    far_final = me - 2 + 4 * odd
    far = (me + n - 4 + 8 * odd) % n
    side_final = me - 1 + 2 * core
    up = (me + 1) % n
    down = (me + n - 1) % n

    barrier = pltpu.get_barrier_semaphore()
    partners = (up, down, near, (me + 4) % n, (me + n - 4) % n)
    for other in partners:
        pl.semaphore_signal(barrier, inc=1, device_id=(other,), device_id_type=pl.DeviceIdType.MESH)

    start = ngs[0]
    count = jnp.int32(0)
    for s in range(nold):
        count = count + (ngs[s] >= 0).astype(jnp.int32)

    def held(i, final):
        f, j = lax.div(i, cap), lax.rem(i, cap)
        idx = final * cap + j - start
        mine = (idx >= 0) & (idx < count)
        idx = jnp.clip(idx, 0, nold - 1)
        row = f * span + lax.div(idx, SUB) * (rows * SUB) + lax.rem(idx, SUB)
        got = old[pl.ds(row, rows, stride=SUB), :]
        return jnp.where(mine, got, 0.0).reshape(EDGE, SUB, LANES)

    def link(stream, src, dst, i, target):
        return pltpu.make_async_remote_copy(
            src_ref=src.at[i], dst_ref=dst.at[i],
            send_sem=ssem.at[stream, i], recv_sem=rsem.at[stream, i],
            device_id=(target,), device_id_type=pl.DeviceIdType.MESH)

    def side_link(i):
        return link(0, side_s, side_r, i, sib)

    def pair_link(i):
        return link(1, pair_s, pair_r, i, sib)

    def far_link(i):
        return link(2, far_s, far_r, i, far)

    def near_link(i):
        return link(3, near_s, near_r, i, near)

    side_goes_far = (core + odd) % 2 == 1

    def send_side(i):
        side_s[i] = held(i, side_final)
        side_link(i).start()

    def send_pair(i):
        pair_s[i] = held(i, sib)
        pair_link(i).start()

    def send_far(i):
        side_link(i).wait_recv()
        far_s[i] = held(i, far_final) + jnp.where(side_goes_far, side_r[i], 0.0)
        far_link(i).start()

    def send_near(i):
        far_link(i).wait_recv()
        near_s[i] = held(i, near) + (far_r[i] + jnp.where(side_goes_far, 0.0, side_r[i]))
        near_link(i).start()

    def loop(lo, hi, *bodies):
        def body(i, carry):
            for each in bodies:
                each(i)
            return carry
        lax.fori_loop(lo, hi, body, 0)

    for copy in loads:
        copy.wait()
    pl.semaphore_wait(barrier, len(partners))
    loop(0, items, send_side)
    loop(0, LAG, send_far)
    loop(LAG, items, send_far, lambda i: send_near(i - LAG))
    loop(items - LAG, items, send_near)
    loop(0, items, send_pair)

    def settle(i):
        pair_link(i).wait_recv()
        near_link(i).wait_recv()
        return held(i, me) + (pair_r[i] + near_r[i])

    def settle_field(i):
        fld[0, lax.div(i, cap), lax.rem(i, cap)] = settle(i)

    def settle_mobility(i):
        mob[i - 2 * cap] = settle(i)

    def ghost_links(t):
        return (
            pltpu.make_async_remote_copy(
                src_ref=fld.at[t, :, :, EDGE - 1], dst_ref=ghosts[t].at[0],
                send_sem=hs.at[t, 0], recv_sem=hr.at[t, 0],
                device_id=(up,), device_id_type=pl.DeviceIdType.MESH),
            pltpu.make_async_remote_copy(
                src_ref=fld.at[t, :, :, 0], dst_ref=ghosts[t].at[1],
                send_sem=hs.at[t, 1], recv_sem=hr.at[t, 1],
                device_id=(down,), device_id_type=pl.DeviceIdType.MESH),
        )

    loop(0, 2 * cap, settle_field)
    for copy in ghost_links(0):
        copy.start()
    loop(2 * cap, items, settle_mobility)

    lane = lax.broadcasted_iota(jnp.int32, (SUB, LANES), 1)
    row = lax.broadcasted_iota(jnp.int32, (SUB, LANES), 0)
    z = lane % EDGE
    z_low, z_high = z == 0, z == EDGE - 1
    y_first, y_last = lane < EDGE, lane >= LANES - EDGE
    row_first, row_last = row == 0, row == SUB - 1

    def local(column, b):
        index = nbs[b * 6 + column]
        return lax.rem(jnp.maximum(index, 0), cap), index >= 0

    def advance(t, b, planes):
        at_y0, has_y0 = local(2, b)
        at_y1, has_y1 = local(3, b)
        at_z0, has_z0 = local(4, b)
        at_z1, has_z1 = local(5, b)
        wall_y0 = y_first & row_first & jnp.logical_not(has_y0)
        wall_y1 = y_last & row_last & jnp.logical_not(has_y1)
        wall_z0 = z_low & jnp.logical_not(has_z0)
        wall_z1 = z_high & jnp.logical_not(has_z1)

        def laplacian(f, x, prev_x, here, next_x):
            y0, y1 = fld[t, f, at_y0, x], fld[t, f, at_y1, x]
            z0, z1 = fld[t, f, at_z0, x], fld[t, f, at_z1, x]
            back = pltpu.roll(here, EDGE, 1)
            back_ghost = pltpu.roll(y0, EDGE, 1)
            prev_y = jnp.where(y_first, pltpu.roll(jnp.where(row_last, back_ghost, back), 1, 0), back)
            prev_y = jnp.where(wall_y0, here, prev_y)
            fore = pltpu.roll(here, LANES - EDGE, 1)
            fore_ghost = pltpu.roll(y1, LANES - EDGE, 1)
            next_y = jnp.where(y_last, pltpu.roll(jnp.where(row_first, fore_ghost, fore), SUB - 1, 0), fore)
            next_y = jnp.where(wall_y1, here, next_y)
            prev_z = jnp.where(z_low, pltpu.roll(z0, LANES - (EDGE - 1), 1), pltpu.roll(here, 1, 1))
            prev_z = jnp.where(wall_z0, here, prev_z)
            next_z = jnp.where(z_high, pltpu.roll(z1, EDGE - 1, 1), pltpu.roll(here, LANES - 1, 1))
            next_z = jnp.where(wall_z1, here, next_z)
            return (prev_x + next_x) + (prev_y + next_y) + (prev_z + next_z) - 6.0 * here

        for x, beside in planes:
            phi, conc = fld[t, 0, b, x], fld[t, 1, b, x]
            lapl_phi = laplacian(0, x, beside(0)[0], phi, beside(0)[1])
            lapl_conc = laplacian(1, x, beside(1)[0], conc, beside(1)[1])
            wetting = 1.0 - phi * phi
            drive = lapl_phi + phi - phi * phi * phi - coupling * conc * wetting * wetting
            new_phi = phi + time_step * mob[b, x] * drive
            new_conc = conc + time_step * lapl_conc + 0.5 * (new_phi - phi)
            if t == STEPS - 1:
                at = lax.div(b, SUB) * (rows * SUB) + lax.rem(b, SUB) + x * (SUB * SUB)
                phi_out[pl.ds(at, SUB, stride=SUB), :] = new_phi
                conc_out[pl.ds(at, SUB, stride=SUB), :] = new_conc
            else:
                fld[t + 1, 0, b, x] = new_phi
                fld[t + 1, 1, b, x] = new_conc

    inner = 3 if (EDGE - 2) % 3 == 0 else 1
    for t in range(STEPS):
        for copy in ghost_links(t):
            copy.wait_recv()

        def ends(b):
            at_x0, has_x0 = local(0, b)
            at_x1, has_x1 = local(1, b)

            def low(f):
                return (jnp.where(has_x0, ghosts[t][0, f, at_x0], fld[t, f, b, 0]), fld[t, f, b, 1])

            def high(f):
                return (fld[t, f, b, EDGE - 2],
                        jnp.where(has_x1, ghosts[t][1, f, at_x1], fld[t, f, b, EDGE - 1]))

            advance(t, b, ((0, low), (EDGE - 1, high)))

        def middle(b):
            def some(k, carry):
                planes = []
                for u in range(inner):
                    x = 1 + k * inner + u
                    planes.append((x, lambda f, x=x: (fld[t, f, b, x - 1], fld[t, f, b, x + 1])))
                advance(t, b, planes)
                return carry
            lax.fori_loop(0, (EDGE - 2) // inner, some, 0)

        loop(0, cap, ends)
        if t + 1 < STEPS:
            for copy in ghost_links(t + 1):
                copy.start()
        loop(0, cap, middle)

    def sent(i):
        side_link(i).wait_send()
        pair_link(i).wait_send()
        far_link(i).wait_send()
        near_link(i).wait_send()

    loop(0, items, sent)
    for t in range(STEPS):
        for copy in ghost_links(t):
            copy.wait_send()


def on_device(n, old_phase, old_solute, old_mobility, new_global_slot, neighbors):
    cap = neighbors.shape[0]
    nold, cells = old_phase.shape
    rows = cells // LANES
    items = FIELDS * cap

    def tiled(field):
        split = field.reshape(nold // SUB, SUB, rows, LANES)
        return split.transpose(0, 2, 1, 3).reshape(nold * rows, LANES)

    def flat(field):
        split = field.reshape(cap // SUB, rows, SUB, LANES)
        return split.transpose(0, 2, 1, 3).reshape(cap, cells)

    buffer = pltpu.VMEM((items, EDGE, SUB, LANES), jnp.float32)
    out = jax.ShapeDtypeStruct((cap * rows, LANES), jnp.float32)
    phase, solute = pl.pallas_call(
        functools.partial(kernel, n, cap, nold),
        out_shape=(out, out),
        in_specs=[pl.BlockSpec(memory_space=pltpu.SMEM)] * 2 + [pl.BlockSpec(memory_space=pl.ANY)] * 3,
        out_specs=[pl.BlockSpec(memory_space=pltpu.VMEM)] * 2,
        scratch_shapes=[pltpu.VMEM((FIELDS * nold * rows, LANES), jnp.float32)] + [buffer] * 8 + [
            pltpu.VMEM((STEPS, 2, cap, EDGE, SUB, LANES), jnp.float32),
            pltpu.VMEM((cap, EDGE, SUB, LANES), jnp.float32),
        ] + [pltpu.VMEM((2, 2, cap, SUB, LANES), jnp.float32)] * STEPS + [
            pltpu.SemaphoreType.DMA((FIELDS,)),
            pltpu.SemaphoreType.DMA((4, items)),
            pltpu.SemaphoreType.DMA((4, items)),
            pltpu.SemaphoreType.DMA((STEPS, 2)),
            pltpu.SemaphoreType.DMA((STEPS, 2)),
        ],
        compiler_params=pltpu.CompilerParams(
            collective_id=0, has_side_effects=True, vmem_limit_bytes=56 * 1024 * 1024),
    )(new_global_slot, neighbors.reshape(-1), tiled(old_phase), tiled(old_solute), tiled(old_mobility))
    return flat(phase), flat(solute)


def solution(mesh):
    placed = (P("blk", None), P("blk", None), P("blk", None), P("blk"), P("blk", None))
    return jax.shard_map(
        functools.partial(on_device, mesh.shape["blk"]),
        mesh=mesh,
        in_specs=placed,
        out_specs=(P("blk", None), P("blk", None)),
        check_vma=False,
    )
```

profile of v0, /device:TPU:0, one launch (start us, length us, event | category | flops | bytes accessed | tf_op | source)
XLA Modules:
  0.0 152.2 jit_solution(12946549092348662791)
XLA Ops:
  0.6 1.3 reshape.37.nbs
  1.9 146.9 %shard_map.68 = (f32[2048,128]{1,0:T(8,128)}, f32[2048,128]{1,0:T(8,128)}) custom-call(s32[16]{0:T(128)} %ngs.1, s32[48]{0:T(128)} %reshape.37.nbs, f32[4096,128]{1,0:T(8,128)} %bitcast.25, f32[4096,128]{1,0:T(8,128)} %bitcast.26, f32[4096,128]{1,0:T(8,128)} %bitcast.27), custom_call_target="tpu_custom_call" | custom-call | tf_op jit(solution)/shard_map/pallas_call | solution.py:263
  148.9 0.0 copy-start
  148.9 2.4 %copy.9 = f32[8,32768]{1,0:T(8,128)} copy(f32[8,32768]{1,0:T(8,128)} %bitcast.29) | data formatting | bytes 2097152
  151.2 0.0 copy-done
  151.2 1.0 copy.10
Async XLA Ops:
  148.9 2.4 %copy-start = (f32[2048,128]{1,0:T(8,128)S(1)}, f32[2048,128]{1,0:T(8,128)}, u32[]{:S(2)}) copy-start(f32[2048,128]{1,0:T(8,128)} %get-tuple-element.5) | copy-start | bytes 3145732
where the time goes:
time: 152 us
  Pallas kernels  147 us (97%)
  local copies, waits for them, and re-layouts  4.6 us (3%)
    pallas_call x1, Pallas kernels, on_device(): pl.pallas_call(functools.partial(kernel, n, cap, nold), out_shape=(out, o...  147 us
    unnamed x4, local copies, waits for them, and re-layouts  3.32 us

commit v1 on v0

--- a/solution.py
+++ b/solution.py
@@ -13,6 +13,8 @@
 SUB = 8
 LANES = 128
 LAG = 3
+AHEAD = 2
+INNER = 5
 
 time_step = 0.15
 coupling = 1.5
@@ -20,7 +22,8 @@
 
 def kernel(n, cap, nold, ngs, nbs, op, oc, om, phi_out, conc_out, old,
            side_s, side_r, pair_s, pair_r, far_s, far_r, near_s, near_r,
-           fld, mob, ghost0, ghost1, ghost2, lsem, ssem, rsem, hs, hr):
+           fld0, fld1, fld2, mob, ghost0, ghost1, ghost2, lsem, ssem, rsem, hs, hr):
+    flds = (fld0, fld1, fld2)
     ghosts = (ghost0, ghost1, ghost2)
     rows = EDGE * SUB
     span = nold * rows
@@ -107,14 +110,17 @@
             return carry
         lax.fori_loop(lo, hi, body, 0)
 
-    for copy in loads:
-        copy.wait()
-    pl.semaphore_wait(barrier, len(partners))
-    loop(0, items, send_side)
-    loop(0, LAG, send_far)
-    loop(LAG, items, send_far, lambda i: send_near(i - LAG))
-    loop(items - LAG, items, send_near)
-    loop(0, items, send_pair)
+    def pipeline(stages, hooks):
+        cuts = set(hooks)
+        for _, offset, size in stages:
+            cuts |= {offset, offset + size}
+        cuts = sorted(cuts)
+        for lo, hi in zip(cuts, cuts[1:] + cuts[-1:]):
+            for act in hooks.get(lo, ()):
+                act()
+            active = [(body, offset) for body, offset, size in stages if offset <= lo and hi <= offset + size]
+            if lo < hi and active:
+                loop(lo, hi, *[lambda i, body=body, offset=offset: body(i - offset) for body, offset in active])
 
     def settle(i):
         pair_link(i).wait_recv()
@@ -122,115 +128,149 @@
         return held(i, me) + (pair_r[i] + near_r[i])
 
     def settle_field(i):
-        fld[0, lax.div(i, cap), lax.rem(i, cap)] = settle(i)
-
-    def settle_mobility(i):
-        mob[i - 2 * cap] = settle(i)
+        flds[0][lax.div(i, cap), lax.rem(i, cap)] = settle(i)
+
+    def settle_mobility(b):
+        mobility = settle(b + 2 * cap)
+        mob[b] = mobility
+        phi = flds[0][0, b]
+        new_phi = phi + time_step * mobility * flds[1][0, b]
+        flds[1][0, b] = new_phi
+        flds[1][1, b] = flds[1][1, b] + 0.5 * (new_phi - phi)
 
     def ghost_links(t):
         return (
             pltpu.make_async_remote_copy(
-                src_ref=fld.at[t, :, :, EDGE - 1], dst_ref=ghosts[t].at[0],
+                src_ref=flds[t].at[:, :, EDGE - 1], dst_ref=ghosts[t].at[0],
                 send_sem=hs.at[t, 0], recv_sem=hr.at[t, 0],
                 device_id=(up,), device_id_type=pl.DeviceIdType.MESH),
             pltpu.make_async_remote_copy(
-                src_ref=fld.at[t, :, :, 0], dst_ref=ghosts[t].at[1],
+                src_ref=flds[t].at[:, :, 0], dst_ref=ghosts[t].at[1],
                 send_sem=hs.at[t, 1], recv_sem=hr.at[t, 1],
                 device_id=(down,), device_id_type=pl.DeviceIdType.MESH),
         )
 
-    loop(0, 2 * cap, settle_field)
-    for copy in ghost_links(0):
-        copy.start()
-    loop(2 * cap, items, settle_mobility)
+    def start_ghosts(t):
+        for copy in ghost_links(t):
+            copy.start()
+
+    def await_ghosts(t):
+        for copy in ghost_links(t):
+            copy.wait_recv()
 
     lane = lax.broadcasted_iota(jnp.int32, (SUB, LANES), 1)
     row = lax.broadcasted_iota(jnp.int32, (SUB, LANES), 0)
     z = lane % EDGE
     z_low, z_high = z == 0, z == EDGE - 1
     y_first, y_last = lane < EDGE, lane >= LANES - EDGE
-    row_first, row_last = row == 0, row == SUB - 1
+    y_start, y_end = y_first & (row == 0), y_last & (row == SUB - 1)
 
     def local(column, b):
-        index = nbs[b * 6 + column]
+        index = nbs[b, column]
         return lax.rem(jnp.maximum(index, 0), cap), index >= 0
 
     def advance(t, b, planes):
+        fld = flds[t]
         at_y0, has_y0 = local(2, b)
         at_y1, has_y1 = local(3, b)
-        at_z0, has_z0 = local(4, b)
-        at_z1, has_z1 = local(5, b)
-        wall_y0 = y_first & row_first & jnp.logical_not(has_y0)
-        wall_y1 = y_last & row_last & jnp.logical_not(has_y1)
-        wall_z0 = z_low & jnp.logical_not(has_z0)
-        wall_z1 = z_high & jnp.logical_not(has_z1)
+        at_z0, _ = local(4, b)
+        at_z1, _ = local(5, b)
+        wall_y0 = y_start & jnp.logical_not(has_y0)
+        wall_y1 = y_end & jnp.logical_not(has_y1)
 
         def laplacian(f, x, prev_x, here, next_x):
-            y0, y1 = fld[t, f, at_y0, x], fld[t, f, at_y1, x]
-            z0, z1 = fld[t, f, at_z0, x], fld[t, f, at_z1, x]
-            back = pltpu.roll(here, EDGE, 1)
-            back_ghost = pltpu.roll(y0, EDGE, 1)
-            prev_y = jnp.where(y_first, pltpu.roll(jnp.where(row_last, back_ghost, back), 1, 0), back)
+            y0, y1 = fld[f, at_y0, x], fld[f, at_y1, x]
+            z0, z1 = fld[f, at_z0, x], fld[f, at_z1, x]
+            back = pltpu.roll(jnp.where(y_end, y0, here), EDGE, 1)
+            prev_y = jnp.where(y_first, pltpu.roll(back, 1, 0), back)
             prev_y = jnp.where(wall_y0, here, prev_y)
-            fore = pltpu.roll(here, LANES - EDGE, 1)
-            fore_ghost = pltpu.roll(y1, LANES - EDGE, 1)
-            next_y = jnp.where(y_last, pltpu.roll(jnp.where(row_first, fore_ghost, fore), SUB - 1, 0), fore)
+            fore = pltpu.roll(jnp.where(y_start, y1, here), LANES - EDGE, 1)
+            next_y = jnp.where(y_last, pltpu.roll(fore, SUB - 1, 0), fore)
             next_y = jnp.where(wall_y1, here, next_y)
             prev_z = jnp.where(z_low, pltpu.roll(z0, LANES - (EDGE - 1), 1), pltpu.roll(here, 1, 1))
-            prev_z = jnp.where(wall_z0, here, prev_z)
             next_z = jnp.where(z_high, pltpu.roll(z1, EDGE - 1, 1), pltpu.roll(here, LANES - 1, 1))
-            next_z = jnp.where(wall_z1, here, next_z)
             return (prev_x + next_x) + (prev_y + next_y) + (prev_z + next_z) - 6.0 * here
 
+        results = []
         for x, beside in planes:
-            phi, conc = fld[t, 0, b, x], fld[t, 1, b, x]
+            phi, conc = fld[0, b, x], fld[1, b, x]
             lapl_phi = laplacian(0, x, beside(0)[0], phi, beside(0)[1])
             lapl_conc = laplacian(1, x, beside(1)[0], conc, beside(1)[1])
             wetting = 1.0 - phi * phi
             drive = lapl_phi + phi - phi * phi * phi - coupling * conc * wetting * wetting
+            new_conc = conc + time_step * lapl_conc
+            if t == 0:
+                results.append((x, drive, new_conc))
+                continue
             new_phi = phi + time_step * mob[b, x] * drive
-            new_conc = conc + time_step * lapl_conc + 0.5 * (new_phi - phi)
+            results.append((x, new_phi, new_conc + 0.5 * (new_phi - phi)))
+        for x, new_phi, new_conc in results:
             if t == STEPS - 1:
                 at = lax.div(b, SUB) * (rows * SUB) + lax.rem(b, SUB) + x * (SUB * SUB)
                 phi_out[pl.ds(at, SUB, stride=SUB), :] = new_phi
                 conc_out[pl.ds(at, SUB, stride=SUB), :] = new_conc
             else:
-                fld[t + 1, 0, b, x] = new_phi
-                fld[t + 1, 1, b, x] = new_conc
-
-    inner = 3 if (EDGE - 2) % 3 == 0 else 1
-    for t in range(STEPS):
-        for copy in ghost_links(t):
-            copy.wait_recv()
-
-        def ends(b):
-            at_x0, has_x0 = local(0, b)
-            at_x1, has_x1 = local(1, b)
-
-            def low(f):
-                return (jnp.where(has_x0, ghosts[t][0, f, at_x0], fld[t, f, b, 0]), fld[t, f, b, 1])
-
-            def high(f):
-                return (fld[t, f, b, EDGE - 2],
-                        jnp.where(has_x1, ghosts[t][1, f, at_x1], fld[t, f, b, EDGE - 1]))
-
-            advance(t, b, ((0, low), (EDGE - 1, high)))
-
-        def middle(b):
-            def some(k, carry):
-                planes = []
-                for u in range(inner):
-                    x = 1 + k * inner + u
-                    planes.append((x, lambda f, x=x: (fld[t, f, b, x - 1], fld[t, f, b, x + 1])))
-                advance(t, b, planes)
-                return carry
-            lax.fori_loop(0, (EDGE - 2) // inner, some, 0)
-
-        loop(0, cap, ends)
+                flds[t + 1][0, b, x] = new_phi
+                flds[t + 1][1, b, x] = new_conc
+
+    inner = max(k for k in range(1, INNER + 1) if (EDGE - 2) % k == 0)
+
+    def ends(t, b):
+        at_x0, has_x0 = local(0, b)
+        at_x1, has_x1 = local(1, b)
+        fld = flds[t]
+
+        def low(f):
+            return (jnp.where(has_x0, ghosts[t][0, f, at_x0], fld[f, b, 0]), fld[f, b, 1])
+
+        def high(f):
+            return (fld[f, b, EDGE - 2], jnp.where(has_x1, ghosts[t][1, f, at_x1], fld[f, b, EDGE - 1]))
+
+        advance(t, b, ((0, low), (EDGE - 1, high)))
+
+    def middle(t, b):
+        fld = flds[t]
+
+        def some(k, carry):
+            planes = []
+            for u in range(inner):
+                x = 1 + k * inner + u
+                planes.append((x, lambda f, x=x: (fld[f, b, x - 1], fld[f, b, x + 1])))
+            advance(t, b, planes)
+            return carry
+        lax.fori_loop(0, (EDGE - 2) // inner, some, 0)
+
+    def prepare(b):
+        ends(0, b)
+        middle(0, b)
+
+    for copy in loads:
+        copy.wait()
+    pl.semaphore_wait(barrier, len(partners))
+    far_at = AHEAD
+    near_at = far_at + LAG
+    settle_at = near_at + LAG + 1
+    ghosts_at = settle_at + 2 * cap
+    pipeline(
+        (
+            (send_side, 0, items),
+            (send_far, far_at, items),
+            (send_near, near_at, items),
+            (send_pair, near_at, items),
+            (settle_field, settle_at, 2 * cap),
+        ),
+        {ghosts_at: (lambda: start_ghosts(0),)},
+    )
+    await_ghosts(0)
+    loop(0, cap, prepare)
+    loop(0, cap, settle_mobility)
+    start_ghosts(1)
+    for t in range(1, STEPS):
+        loop(0, cap, functools.partial(middle, t))
+        await_ghosts(t)
+        loop(0, cap, functools.partial(ends, t))
         if t + 1 < STEPS:
-            for copy in ghost_links(t + 1):
-                copy.start()
-        loop(0, cap, middle)
+            start_ghosts(t + 1)
 
     def sent(i):
         side_link(i).wait_send()
@@ -266,7 +306,7 @@
         in_specs=[pl.BlockSpec(memory_space=pltpu.SMEM)] * 2 + [pl.BlockSpec(memory_space=pl.ANY)] * 3,
         out_specs=[pl.BlockSpec(memory_space=pltpu.VMEM)] * 2,
         scratch_shapes=[pltpu.VMEM((FIELDS * nold * rows, LANES), jnp.float32)] + [buffer] * 8 + [
-            pltpu.VMEM((STEPS, 2, cap, EDGE, SUB, LANES), jnp.float32),
+            pltpu.VMEM((2, cap, EDGE, SUB, LANES), jnp.float32)] * STEPS + [
             pltpu.VMEM((cap, EDGE, SUB, LANES), jnp.float32),
         ] + [pltpu.VMEM((2, 2, cap, SUB, LANES), jnp.float32)] * STEPS + [
             pltpu.SemaphoreType.DMA((FIELDS,)),
@@ -277,7 +317,7 @@
         ],
         compiler_params=pltpu.CompilerParams(
             collective_id=0, has_side_effects=True, vmem_limit_bytes=56 * 1024 * 1024),
-    )(new_global_slot, neighbors.reshape(-1), tiled(old_phase), tiled(old_solute), tiled(old_mobility))
+    )(new_global_slot, neighbors, tiled(old_phase), tiled(old_solute), tiled(old_mobility))
     return flat(phase), flat(solute)
 
 

time: 152 us -> 111 us (0.73)
  Pallas kernels: 147 us -> 107 us
    pallas_call x1, Pallas kernels: 147 us -> 107 us  [on_device(): pl.pallas_call(functools.partial(kernel, n, cap, nold), out_shape=(out, o...]
where the time goes in v1:
time: 111 us
  Pallas kernels  107 us (96%)
  local copies, waits for them, and re-layouts  3.32 us (3%)
    pallas_call x1, Pallas kernels, on_device(): pl.pallas_call(functools.partial(kernel, n, cap, nold), out_shape=(out, o...  107 us
    unnamed x4, local copies, waits for them, and re-layouts  3.32 us

profile of v1, /device:TPU:0, one launch (start us, length us, event | category | flops | bytes accessed | tf_op | source)
XLA Modules:
  0.0 110.7 jit_solution(1188415158089352043)
XLA Ops:
  0.6 106.7 %shard_map.68 = (f32[2048,128]{1,0:T(8,128)}, f32[2048,128]{1,0:T(8,128)}) custom-call(s32[16]{0:T(128)} %ngs.1, s32[8,6]{1,0:T(8,128)} %nbs.1, f32[4096,128]{1,0:T(8,128)} %bitcast.25, f32[4096,128]{1,0:T(8,128)} %bitcast.26, f32[4096,128]{1,0:T(8,128)} %bitcast.27), custom_call_target="tpu_custom_call" | custom-call | tf_op jit(solution)/shard_map/pallas_call | solution.py:303
  107.3 0.0 copy-start
  107.3 2.4 %copy.9 = f32[8,32768]{1,0:T(8,128)} copy(f32[8,32768]{1,0:T(8,128)} %bitcast.29) | data formatting | bytes 2097152
  109.7 0.0 copy-done
  109.7 1.0 copy.10
Async XLA Ops:
  107.3 2.4 %copy-start = (f32[2048,128]{1,0:T(8,128)S(1)}, f32[2048,128]{1,0:T(8,128)}, u32[]{:S(2)}) copy-start(f32[2048,128]{1,0:T(8,128)} %get-tuple-element.5) | copy-start | bytes 3145732

commit v2 on v1

--- a/solution.py
+++ b/solution.py
@@ -12,9 +12,11 @@
 FIELDS = 3
 SUB = 8
 LANES = 128
-LAG = 3
+PARTS = 2
+LAG = 4
 AHEAD = 2
-INNER = 5
+SETTLE = 4
+INNER = 10
 
 time_step = 0.15
 coupling = 1.5
@@ -27,7 +29,8 @@
     ghosts = (ghost0, ghost1, ghost2)
     rows = EDGE * SUB
     span = nold * rows
-    items = FIELDS * cap
+    part = rows // PARTS
+    items = FIELDS * cap * PARTS
     loads = [
         pltpu.make_async_copy(src, old.at[pl.ds(f * span, span)], lsem.at[f])
         for f, src in enumerate((op, oc, om))
@@ -41,29 +44,43 @@
     sib = me + 1 - 2 * core
     near = me + 2 - 4 * odd
     far_final = me - 2 + 4 * odd
-    far = (me + n - 4 + 8 * odd) % n
+    far = me - 4 + 8 * odd
+    far_source = me + 4 - 8 * odd
     side_final = me - 1 + 2 * core
-    up = (me + 1) % n
-    down = (me + n - 1) % n
+    up, down = me + 1, me - 1
+    has_up, has_down = up < n, down >= 0
+    sends_far = (far_final >= 0) & (far_final < n)
+    gets_far = (far_source >= 0) & (far_source < n)
 
     barrier = pltpu.get_barrier_semaphore()
-    partners = (up, down, near, (me + 4) % n, (me + n - 4) % n)
-    for other in partners:
-        pl.semaphore_signal(barrier, inc=1, device_id=(other,), device_id_type=pl.DeviceIdType.MESH)
+    expected = jnp.int32(0)
+    for other, there in ((up, has_up), (down, has_down), (near, None), (far, sends_far), (far_source, gets_far)):
+        def greet(other=other):
+            pl.semaphore_signal(barrier, inc=1, device_id=(other,), device_id_type=pl.DeviceIdType.MESH)
+        if there is None:
+            greet()
+            expected = expected + 1
+        else:
+            pl.when(there)(greet)
+            expected = expected + there.astype(jnp.int32)
 
     start = ngs[0]
     count = jnp.int32(0)
     for s in range(nold):
         count = count + (ngs[s] >= 0).astype(jnp.int32)
 
+    def place(i):
+        block = lax.div(i, PARTS)
+        return lax.div(block, cap), lax.rem(block, cap), lax.rem(i, PARTS)
+
     def held(i, final):
-        f, j = lax.div(i, cap), lax.rem(i, cap)
+        f, j, h = place(i)
         idx = final * cap + j - start
         mine = (idx >= 0) & (idx < count)
         idx = jnp.clip(idx, 0, nold - 1)
-        row = f * span + lax.div(idx, SUB) * (rows * SUB) + lax.rem(idx, SUB)
-        got = old[pl.ds(row, rows, stride=SUB), :]
-        return jnp.where(mine, got, 0.0).reshape(EDGE, SUB, LANES)
+        row = f * span + lax.div(idx, SUB) * (rows * SUB) + lax.rem(idx, SUB) + h * (part * SUB)
+        got = old[pl.ds(row, part, stride=SUB), :]
+        return jnp.where(mine, got, 0.0).reshape(EDGE // PARTS, SUB, LANES)
 
     def link(stream, src, dst, i, target):
         return pltpu.make_async_remote_copy(
@@ -93,14 +110,24 @@
         pair_s[i] = held(i, sib)
         pair_link(i).start()
 
+    def add_side(i, total):
+        side_link(i).wait_recv()
+        total[i] += side_r[i]
+
     def send_far(i):
-        side_link(i).wait_recv()
-        far_s[i] = held(i, far_final) + jnp.where(side_goes_far, side_r[i], 0.0)
-        far_link(i).start()
+        far_s[i] = held(i, far_final)
+        pl.when(side_goes_far)(lambda: add_side(i, far_s))
+        pl.when(sends_far)(lambda: far_link(i).start())
 
     def send_near(i):
-        far_link(i).wait_recv()
-        near_s[i] = held(i, near) + (far_r[i] + jnp.where(side_goes_far, 0.0, side_r[i]))
+        near_s[i] = held(i, near)
+        pl.when(jnp.logical_not(side_goes_far))(lambda: add_side(i, near_s))
+
+        @pl.when(gets_far)
+        def add_far():
+            far_link(i).wait_recv()
+            near_s[i] += far_r[i]
+
         near_link(i).start()
 
     def loop(lo, hi, *bodies):
@@ -128,35 +155,37 @@
         return held(i, me) + (pair_r[i] + near_r[i])
 
     def settle_field(i):
-        flds[0][lax.div(i, cap), lax.rem(i, cap)] = settle(i)
-
-    def settle_mobility(b):
-        mobility = settle(b + 2 * cap)
-        mob[b] = mobility
-        phi = flds[0][0, b]
-        new_phi = phi + time_step * mobility * flds[1][0, b]
-        flds[1][0, b] = new_phi
-        flds[1][1, b] = flds[1][1, b] + 0.5 * (new_phi - phi)
-
-    def ghost_links(t):
-        return (
-            pltpu.make_async_remote_copy(
-                src_ref=flds[t].at[:, :, EDGE - 1], dst_ref=ghosts[t].at[0],
-                send_sem=hs.at[t, 0], recv_sem=hr.at[t, 0],
-                device_id=(up,), device_id_type=pl.DeviceIdType.MESH),
-            pltpu.make_async_remote_copy(
-                src_ref=flds[t].at[:, :, 0], dst_ref=ghosts[t].at[1],
-                send_sem=hs.at[t, 1], recv_sem=hr.at[t, 1],
-                device_id=(down,), device_id_type=pl.DeviceIdType.MESH),
-        )
+        f, j, h = place(i)
+        planes = pl.ds(h * (EDGE // PARTS), EDGE // PARTS)
+        flds[0][f, j, planes] = settle(i)
+
+    def settle_mobility(i):
+        _, b, h = place(i)
+        planes = pl.ds(h * (EDGE // PARTS), EDGE // PARTS)
+        mobility = settle(i + 2 * cap * PARTS)
+        mob[b, planes] = mobility
+        phi = flds[0][0, b, planes]
+        new_phi = phi + time_step * mobility * flds[1][0, b, planes]
+        flds[1][0, b, planes] = new_phi
+        flds[1][1, b, planes] = flds[1][1, b, planes] + 0.5 * (new_phi - phi)
+
+    def ghost_link(t, side):
+        return pltpu.make_async_remote_copy(
+            src_ref=flds[t].at[:, :, 0 if side else EDGE - 1], dst_ref=ghosts[t].at[side],
+            send_sem=hs.at[t, side], recv_sem=hr.at[t, side],
+            device_id=(down if side else up,), device_id_type=pl.DeviceIdType.MESH)
 
     def start_ghosts(t):
-        for copy in ghost_links(t):
-            copy.start()
+        pl.when(has_up)(lambda: ghost_link(t, 0).start())
+        pl.when(has_down)(lambda: ghost_link(t, 1).start())
 
     def await_ghosts(t):
-        for copy in ghost_links(t):
-            copy.wait_recv()
+        pl.when(has_down)(lambda: ghost_link(t, 0).wait_recv())
+        pl.when(has_up)(lambda: ghost_link(t, 1).wait_recv())
+
+    def await_sent(t):
+        pl.when(has_up)(lambda: ghost_link(t, 0).wait_send())
+        pl.when(has_down)(lambda: ghost_link(t, 1).wait_send())
 
     lane = lax.broadcasted_iota(jnp.int32, (SUB, LANES), 1)
     row = lax.broadcasted_iota(jnp.int32, (SUB, LANES), 0)
@@ -246,24 +275,24 @@
 
     for copy in loads:
         copy.wait()
-    pl.semaphore_wait(barrier, len(partners))
-    far_at = AHEAD
-    near_at = far_at + LAG
-    settle_at = near_at + LAG + 1
-    ghosts_at = settle_at + 2 * cap
+    pl.semaphore_wait(barrier, expected)
+    fields = 2 * cap * PARTS
+    near_at = AHEAD + LAG
+    settle_at = near_at + SETTLE
+    ghosts_at = settle_at + fields
+    prepare_at = ghosts_at + 2
     pipeline(
         (
             (send_side, 0, items),
-            (send_far, far_at, items),
+            (send_far, AHEAD, items),
             (send_near, near_at, items),
             (send_pair, near_at, items),
-            (settle_field, settle_at, 2 * cap),
+            (settle_field, settle_at, fields),
+            (prepare, prepare_at, cap),
+            (settle_mobility, prepare_at + 1, cap * PARTS),
         ),
-        {ghosts_at: (lambda: start_ghosts(0),)},
+        {ghosts_at: (lambda: start_ghosts(0),), prepare_at: (lambda: await_ghosts(0),)},
     )
-    await_ghosts(0)
-    loop(0, cap, prepare)
-    loop(0, cap, settle_mobility)
     start_ghosts(1)
     for t in range(1, STEPS):
         loop(0, cap, functools.partial(middle, t))
@@ -275,20 +304,19 @@
     def sent(i):
         side_link(i).wait_send()
         pair_link(i).wait_send()
-        far_link(i).wait_send()
+        pl.when(sends_far)(lambda: far_link(i).wait_send())
         near_link(i).wait_send()
 
     loop(0, items, sent)
     for t in range(STEPS):
-        for copy in ghost_links(t):
-            copy.wait_send()
+        await_sent(t)
 
 
 def on_device(n, old_phase, old_solute, old_mobility, new_global_slot, neighbors):
     cap = neighbors.shape[0]
     nold, cells = old_phase.shape
     rows = cells // LANES
-    items = FIELDS * cap
+    items = FIELDS * cap * PARTS
 
     def tiled(field):
         split = field.reshape(nold // SUB, SUB, rows, LANES)
@@ -298,7 +326,7 @@
         split = field.reshape(cap // SUB, rows, SUB, LANES)
         return split.transpose(0, 2, 1, 3).reshape(cap, cells)
 
-    buffer = pltpu.VMEM((items, EDGE, SUB, LANES), jnp.float32)
+    buffer = pltpu.VMEM((items, EDGE // PARTS, SUB, LANES), jnp.float32)
     out = jax.ShapeDtypeStruct((cap * rows, LANES), jnp.float32)
     phase, solute = pl.pallas_call(
         functools.partial(kernel, n, cap, nold),

time: 111 us -> 101 us (0.910)
  Pallas kernels: 107 us -> 97.1 us
    pallas_call x1, Pallas kernels: 107 us -> 97.1 us  [on_device(): pl.pallas_call(functools.partial(kernel, n, cap, nold), out_shape=(out, o...]
where the time goes in v2:
time: 101 us
  Pallas kernels  97.1 us (96%)
  local copies, waits for them, and re-layouts  3.32 us (3%)
    pallas_call x1, Pallas kernels, on_device(): pl.pallas_call(functools.partial(kernel, n, cap, nold), out_shape=(out, o...  97.1 us
    unnamed x4, local copies, waits for them, and re-layouts  3.32 us

profile of v2, /device:TPU:0, one launch (start us, length us, event | category | flops | bytes accessed | tf_op | source)
XLA Modules:
  0.0 101.1 jit_solution(6239567951275322374)
XLA Ops:
  0.6 97.1 %shard_map.68 = (f32[2048,128]{1,0:T(8,128)}, f32[2048,128]{1,0:T(8,128)}) custom-call(s32[16]{0:T(128)} %ngs.1, s32[8,6]{1,0:T(8,128)} %nbs.1, f32[4096,128]{1,0:T(8,128)} %bitcast.25, f32[4096,128]{1,0:T(8,128)} %bitcast.26, f32[4096,128]{1,0:T(8,128)} %bitcast.27), custom_call_target="tpu_custom_call" | custom-call | tf_op jit(solution)/shard_map/pallas_call | solution.py:331
  97.8 0.0 copy-start
  97.8 2.4 %copy.9 = f32[8,32768]{1,0:T(8,128)} copy(f32[8,32768]{1,0:T(8,128)} %bitcast.29) | data formatting | bytes 2097152
  100.1 0.0 copy-done
  100.1 1.0 copy.10
Async XLA Ops:
  97.8 2.4 %copy-start = (f32[2048,128]{1,0:T(8,128)S(1)}, f32[2048,128]{1,0:T(8,128)}, u32[]{:S(2)}) copy-start(f32[2048,128]{1,0:T(8,128)} %get-tuple-element.5) | copy-start | bytes 3145732

commit v3 on v2

--- a/solution.py
+++ b/solution.py
@@ -12,11 +12,11 @@
 FIELDS = 3
 SUB = 8
 LANES = 128
-PARTS = 2
-LAG = 4
+PARTS = 1
+LAG = 2
 AHEAD = 2
-SETTLE = 4
-INNER = 10
+SETTLE = 2
+INNER = 15
 
 time_step = 0.15
 coupling = 1.5
@@ -280,7 +280,7 @@
     near_at = AHEAD + LAG
     settle_at = near_at + SETTLE
     ghosts_at = settle_at + fields
-    prepare_at = ghosts_at + 2
+    prepare_at = ghosts_at + 1
     pipeline(
         (
             (send_side, 0, items),

time: 101 us -> 99.4 us (0.984)
  Pallas kernels: 97.1 us -> 95.3 us
    pallas_call x1, Pallas kernels: 97.1 us -> 95.3 us  [on_device(): pl.pallas_call(functools.partial(kernel, n, cap, nold), out_shape=(out, o...]
where the time goes in v3:
time: 99.4 us; the launch traced here: 99.2 us
  Pallas kernels  95.3 us (96%)
  local copies, waits for them, and re-layouts  3.32 us (3%)
    pallas_call x1, Pallas kernels, on_device(): pl.pallas_call(functools.partial(kernel, n, cap, nold), out_shape=(out, o...  95.3 us
    unnamed x4, local copies, waits for them, and re-layouts  3.32 us

profile of v3, /device:TPU:0, one launch (start us, length us, event | category | flops | bytes accessed | tf_op | source)
XLA Modules:
  0.0 99.2 jit_solution(13552634619036121254)
XLA Ops:
  0.6 95.3 %shard_map.68 = (f32[2048,128]{1,0:T(8,128)}, f32[2048,128]{1,0:T(8,128)}) custom-call(s32[16]{0:T(128)} %ngs.1, s32[8,6]{1,0:T(8,128)} %nbs.1, f32[4096,128]{1,0:T(8,128)} %bitcast.25, f32[4096,128]{1,0:T(8,128)} %bitcast.26, f32[4096,128]{1,0:T(8,128)} %bitcast.27), custom_call_target="tpu_custom_call" | custom-call | tf_op jit(solution)/shard_map/pallas_call | solution.py:331
  95.9 0.0 copy-start
  95.9 2.4 %copy.9 = f32[8,32768]{1,0:T(8,128)} copy(f32[8,32768]{1,0:T(8,128)} %bitcast.29) | data formatting | bytes 2097152
  98.3 0.0 copy-done
  98.3 1.0 copy.10
Async XLA Ops:
  95.9 2.4 %copy-start = (f32[2048,128]{1,0:T(8,128)S(1)}, f32[2048,128]{1,0:T(8,128)}, u32[]{:S(2)}) copy-start(f32[2048,128]{1,0:T(8,128)} %get-tuple-element.5) | copy-start | bytes 3145732
